TPU v7x, 32 devices: a whole 2x2x4 slice. The times are simulated.
32 devices in a mesh: gx: 8 (over z, core), gy: 4 (over y, x).
Axes of the slice: x: 2, y: 2, z: 4, core: 2. Of those that a mesh axis runs over, the one named last changes fastest.
Arguments:
- rhs: float32 [64, 32, 6, 3, 256], P('gx', 'gy'), may hold values from -400 to 400
- contrast: float32 [64, 32, 256], P('gx', 'gy'), may hold values from 0.2 to 2
- occupied: int32 [64, 32], P('gx', 'gy'), may hold values 0 or 1
- near: bfloat16 [5, 768, 768], replicated, may hold values from -0.078125 to 0.078125
- basis: bfloat16 [768, 64], replicated, may hold values from -0.21875 to 0.21875
- transfer: float32 [4, 4, 64, 64], replicated, may hold values from -0.5 to 0.5
- coupling: float32 [5, 20, 64, 64], replicated, may hold values from -0.15625 to 0.15625
Outputs:
- third: float32 [64, 32, 6, 3, 256], P('gx', 'gy')
- hess: float32 [6, 6], replicated
All inputs are finite; a program needn't handle non-finite values. No bound on the sum of `occupied` on one device may be relied on, other than what follows from the above.
Results may differ from a plain program's by a relative error of at most 0.0031.
Values may be sent and summed in bfloat16 or wider, within the bound.
A program may use at most 128 MiB of HBM per device.

v0:
```python
import functools

import jax
import jax.numpy as jnp
from jax import lax
from jax.experimental import pallas as pl
from jax.experimental.pallas import tpu as pltpu
from jax.sharding import PartitionSpec as P

EPSILON = 1e-06
NEAR_BASE = ((0, 0), (1, -1), (1, 0), (1, 1), (0, 1))
AROUND = [(a, b) for a in (-1, 0, 1) for b in (-1, 0, 1)]
COMPASS = [d for d in AROUND if d != (0, 0)]
MESH = pl.DeviceIdType.MESH
VMEM = pl.BlockSpec(memory_space=pltpu.VMEM)


def near_lookup():
    table = {}
    for slot, (a, b) in enumerate(NEAR_BASE):
        table[(a, b)] = (slot, False)
        if (a, b) != (0, 0):
            table[(-a, -b)] = (slot, True)
    return table


def far_lookup():
    base = [
        (a, b)
        for a in range(-3, 4)
        for b in range(-3, 4)
        if max(abs(a), abs(b)) >= 2 and (a > 0 or (a == 0 and b > 0))
    ]
    table = {}
    for slot, (a, b) in enumerate(base):
        table[(a, b)] = (slot, False)
        table[(-a, -b)] = (slot, True)
    return table


def halves(values):
    high = values.astype(jnp.bfloat16)
    return high, (values - high.astype(jnp.float32)).astype(jnp.bfloat16)


def far_kernel(coupling, high, low):
    table = far_lookup()
    rank = coupling.shape[2]
    children = [(c, e) for c in (0, 1) for e in (0, 1)]
    empty = jnp.zeros((rank, rank), jnp.float32)
    row = 0
    for px, py in AROUND:
        for c, e in children:
            line = []
            for tc, te in children:
                found = table.get((2 * px + c - tc, 2 * py + e - te))
                if found is None:
                    line.append(empty)
                else:
                    block = coupling[0, found[0]]
                    line.append(block.T if found[1] else block)
            high[0, row : row + rank, :], low[0, row : row + rank, :] = halves(
                jnp.concatenate(line, axis=1)
            )
            row += rank


def far_matrices(coupling):
    levels, slots, rank, _ = coupling.shape
    spec = pl.BlockSpec((1, 36 * rank, 4 * rank), lambda i: (i, 0, 0))
    shape = jax.ShapeDtypeStruct((levels, 36 * rank, 4 * rank), jnp.bfloat16)
    return pl.pallas_call(
        far_kernel,
        grid=(levels,),
        in_specs=[pl.BlockSpec((1, slots, rank, rank), lambda i: (i, 0, 0, 0))],
        out_specs=[spec, spec],
        out_shape=[shape, shape],
    )(coupling)


def place(index, size_y):
    return {"gx": index // size_y, "gy": index % size_y}


def greet_all(size_x, size_y):
    total = size_x * size_y
    me = lax.axis_index("gx") * size_y + lax.axis_index("gy")
    barrier = pltpu.get_barrier_semaphore()

    def greet(step, carry):
        other = (me + step) % total
        pl.semaphore_signal(
            barrier, inc=1, device_id=place(other, size_y), device_id_type=MESH
        )
        return carry

    lax.fori_loop(1, total, greet, 0)
    pl.semaphore_wait(barrier, total - 1)


def gather_copy(source, target, send, receive, step, size_x, size_y):
    total = size_x * size_y
    me = lax.axis_index("gx") * size_y + lax.axis_index("gy")
    other = (me + step) % total
    return pltpu.make_async_remote_copy(
        src_ref=source,
        dst_ref=target.at[me],
        send_sem=send.at[step],
        recv_sem=receive.at[step],
        device_id=place(other, size_y),
        device_id_type=MESH,
    )


def sum_kernel(size_x, size_y, part, out, slots, send, receive):
    total = size_x * size_y
    me = lax.axis_index("gx") * size_y + lax.axis_index("gy")
    greet_all(size_x, size_y)

    def begin(step, carry):
        gather_copy(part, slots, send, receive, step, size_x, size_y).start()
        return carry

    def finish(step, carry):
        source = (me + total - step) % total
        pltpu.make_async_remote_copy(
            src_ref=part,
            dst_ref=slots.at[source],
            send_sem=send.at[step],
            recv_sem=receive.at[step],
            device_id=place((me + step) % total, size_y),
            device_id_type=MESH,
        ).wait()
        return carry

    lax.fori_loop(1, total, begin, 0)
    slots[me] = part[...]
    lax.fori_loop(1, total, finish, 0)
    out[...] = jnp.sum(slots[...], axis=0)


def sum_all(values, size_x, size_y):
    rows, columns = values.shape
    part = jnp.pad(values, ((0, 8 - rows), (0, 128 - columns)))
    total = size_x * size_y
    summed = pl.pallas_call(
        functools.partial(sum_kernel, size_x, size_y),
        in_specs=[VMEM],
        out_specs=VMEM,
        out_shape=jax.ShapeDtypeStruct((8, 128), jnp.float32),
        scratch_shapes=[
            pltpu.VMEM((total, 8, 128), jnp.float32),
            pltpu.SemaphoreType.DMA((total,)),
            pltpu.SemaphoreType.DMA((total,)),
        ],
        compiler_params=pltpu.CompilerParams(collective_id=0, has_side_effects=True),
    )(part)
    return summed[:rows, :columns]


def strip(move, length):
    if move > 0:
        return pl.ds(length, 1), pl.ds(0, 1)
    if move < 0:
        return pl.ds(1, 1), pl.ds(length + 1, 1)
    return pl.ds(1, length), pl.ds(1, length)


def stacked(values):
    high = values.astype(jnp.bfloat16).astype(jnp.float32)
    return jnp.concatenate([high, values - high], axis=0).astype(jnp.bfloat16)


def product(left, right, across=1):
    return lax.dot_general(
        left, right, (((1,), (1 - across,)), ((), ())), preferred_element_type=jnp.float32
    )


def times(values, high, low, across=1):
    both = stacked(values)
    total = product(both, high, across) + product(both, low, across)
    rows = values.shape[0]
    return total[:rows] + total[rows:]


def group(boxes, size_x, size_y):
    rows = []
    for x in range(0, size_x, 2):
        for y in range(0, size_y, 2):
            four = [(x + c) * size_y + y + e for c in (0, 1) for e in (0, 1)]
            rows.append(jnp.concatenate([boxes[8 * i : 8 * i + 8] for i in four], axis=1))
    return rows


def ungroup(parents, size_x, size_y):
    rank = parents.shape[1] // 4
    rows = []
    for x in range(2 * size_x):
        for y in range(2 * size_y):
            i = (x // 2) * size_y + y // 2
            k = 2 * (x % 2) + y % 2
            rows.append(parents[8 * i : 8 * i + 8, k * rank : (k + 1) * rank])
    return jnp.concatenate(rows, axis=0)


def clear_rim(out):
    long_x, long_y = out.shape[0], out.shape[1]
    line_x = jnp.zeros((1,) + out.shape[1:], out.dtype)
    line_y = jnp.zeros((long_x, 1) + out.shape[2:], out.dtype)
    out[0:1] = line_x
    out[long_x - 1 : long_x] = line_x
    out[:, 0:1] = line_y
    out[:, long_y - 1 : long_y] = line_y


def operate_kernel(size_x, size_y, inner, *refs):
    source, near, basis, lifts, far_high, far_low, out = refs[:7]
    padded = refs[7]
    pyramid = refs[8 : 8 + inner]
    rest = refs[8 + inner :]
    coarse = far_high.shape[0] - inner
    tops = rest[:coarse]
    mine, gathered, shifted, total, send, receive, gather_send, gather_receive = rest[coarse:]
    side = source.shape[0]
    width = source.shape[3]
    rank = basis.shape[1]
    devices = size_x * size_y
    me_x, me_y = lax.axis_index("gx"), lax.axis_index("gy")
    me = me_x * size_y + me_y
    ways = range(len(COMPASS))
    bands = (padded,) + tuple(pyramid)

    for band in bands + tuple(tops):
        clear_rim(band)
    padded[1 : 1 + side, 1 : 1 + side] = source[...]
    greet_all(size_x, size_y)

    def copy_of(number, way):
        move_x, move_y = COMPASS[way]
        band = bands[number]
        from_x, to_x = strip(move_x, band.shape[0] - 2)
        from_y, to_y = strip(move_y, band.shape[1] - 2)
        return pltpu.make_async_remote_copy(
            src_ref=band.at[from_x, from_y],
            dst_ref=band.at[to_x, to_y],
            send_sem=send.at[number, way],
            recv_sem=receive.at[number, way],
            device_id={"gx": me_x + move_x, "gy": me_y + move_y},
            device_id_type=MESH,
        )

    def inside(place_x, place_y):
        return (place_x >= 0) & (place_x < size_x) & (place_y >= 0) & (place_y < size_y)

    def start_bands(numbers):
        for way in ways:
            move_x, move_y = COMPASS[way]

            @pl.when(inside(me_x + move_x, me_y + move_y))
            def _(way=way):
                for number in numbers:
                    copy_of(number, way).start()

    def finish_bands(numbers):
        for way in ways:
            move_x, move_y = COMPASS[way]

            @pl.when(inside(me_x + move_x, me_y + move_y))
            def _(way=way):
                for number in numbers:
                    copy_of(number, way).wait_send()

            @pl.when(inside(me_x - move_x, me_y - move_y))
            def _(way=way):
                for number in numbers:
                    copy_of(number, way).wait_recv()

    start_bands((0,))

    flat = source[...].astype(jnp.float32).reshape(side * side * 8, width).astype(jnp.bfloat16)
    level = product(flat, basis[...])
    span = side
    for depth in range(inner):
        parents = group(level, span, span)
        span //= 2
        for i, parent in enumerate(parents):
            pyramid[depth][1 + i // span, 1 + i % span] = parent
        high, low = halves(lifts[depth])
        level = times(jnp.concatenate(parents, axis=0), high, low)
    mine[...] = level
    gathered[me] = level
    start_bands(range(1, inner + 1))

    def begin(step, carry):
        gather_copy(mine, gathered, gather_send, gather_receive, step, size_x, size_y).start()
        return carry

    lax.fori_loop(1, devices, begin, 0)

    finish_bands((0,))
    for b in range(3):
        shifted[b] = (
            padded[:, b : b + side]
            .astype(jnp.float32)
            .reshape((side + 2) * side * 8, width)
            .astype(jnp.bfloat16)
        )
    rows = side * side * 8
    table = near_lookup()
    chunk = 256 if width % 256 == 0 else 128

    def near_columns(index, carry):
        columns = pl.ds(pl.multiple_of(index * chunk, chunk), chunk)
        value = jnp.zeros((rows, chunk), jnp.float32)
        for a, b in AROUND:
            slot, flipped = table[(a, b)]
            piece = shifted[1 + b, (1 + a) * side * 8 : (1 + a) * side * 8 + rows]
            if flipped:
                value = value + product(piece, near[slot, columns, :], 0)
            else:
                value = value + product(piece, near[slot, :, columns])
        total[:, columns] = value
        return carry

    lax.fori_loop(0, width // chunk, near_columns, 0)
    finish_bands(range(1, inner + 1))

    def finish(step, carry):
        other = (me + devices - step) % devices
        pltpu.make_async_remote_copy(
            src_ref=mine,
            dst_ref=gathered.at[other],
            send_sem=gather_send.at[step],
            recv_sem=gather_receive.at[step],
            device_id=place((me + step) % devices, size_y),
            device_id_type=MESH,
        ).wait()
        return carry

    lax.fori_loop(1, devices, finish, 0)

    def couple(depth, window):
        value = None
        for k, (a, b) in enumerate(AROUND):
            span_rows = slice(4 * rank * k, 4 * rank * (k + 1))
            term = times(window(a, b), far_high[depth, span_rows], far_low[depth, span_rows])
            value = term if value is None else value + term
        return value

    across, along = size_x, size_y
    boxes = gathered[...].reshape(devices * 8, rank)
    for step in range(coarse):
        parents = group(boxes, across, along)
        across, along = across // 2, along // 2
        for i, parent in enumerate(parents):
            tops[step][1 + i // along, 1 + i % along] = parent
        if step < coarse - 1:
            high, low = halves(lifts[inner + step])
            boxes = times(jnp.concatenate(parents, axis=0), high, low)
    down = None
    for step in range(coarse - 1, -1, -1):
        near_x, near_y = me_x >> step + 1, me_y >> step + 1
        value = couple(
            inner + step, lambda a, b: tops[step][near_x + (1 + a), near_y + (1 + b)]
        )
        if down is not None:
            high, low = halves(lifts[inner + step])
            value = value + times(down, high, low, 0)
        child = 2 * (me_x >> step & 1) + (me_y >> step & 1)
        down = jnp.zeros((8, rank), jnp.float32)
        for i in range(4):
            down = jnp.where(child == i, value[:, i * rank : (i + 1) * rank], down)

    span = 1
    for depth in range(inner - 1, -1, -1):
        band = pyramid[depth]
        value = couple(
            depth,
            lambda a, b: band[1 + a : 1 + a + span, 1 + b : 1 + b + span].reshape(
                span * span * 8, 4 * rank
            ),
        )
        high, low = halves(lifts[depth])
        value = value + times(down, high, low, 0)
        down = ungroup(value, span, span)
        span *= 2
    spread_down = product(stacked(down), basis[...], 0)
    out[...] = (total[...] + spread_down[:rows] + spread_down[rows:]).reshape(out.shape)


def apply(source, near, basis, lifts, far_high, far_low, size_x, size_y):
    side, _, _, width = source.shape
    rank = basis.shape[1]
    inner = side.bit_length() - 1
    coarse = far_high.shape[0] - inner
    devices = size_x * size_y
    halos = inner + 1
    scratch = [pltpu.VMEM((side + 2, side + 2, 8, width), jnp.bfloat16)]
    for depth in range(inner):
        span = (side >> depth + 1) + 2
        scratch.append(pltpu.VMEM((span, span, 8, 4 * rank), jnp.float32))
    for step in range(coarse):
        grid = ((size_x >> step + 1) + 2, (size_y >> step + 1) + 2)
        scratch.append(pltpu.VMEM(grid + (8, 4 * rank), jnp.float32))
    scratch += [
        pltpu.VMEM((8, rank), jnp.float32),
        pltpu.VMEM((devices, 8, rank), jnp.float32),
        pltpu.VMEM((3, (side + 2) * side * 8, width), jnp.bfloat16),
        pltpu.VMEM((side * side * 8, width), jnp.float32),
        pltpu.SemaphoreType.DMA((halos, len(COMPASS))),
        pltpu.SemaphoreType.DMA((halos, len(COMPASS))),
        pltpu.SemaphoreType.DMA((devices,)),
        pltpu.SemaphoreType.DMA((devices,)),
    ]
    return pl.pallas_call(
        functools.partial(operate_kernel, size_x, size_y, inner),
        in_specs=[VMEM] * 6,
        out_specs=VMEM,
        out_shape=jax.ShapeDtypeStruct(source.shape, jnp.float32),
        scratch_shapes=scratch,
        compiler_params=pltpu.CompilerParams(collective_id=1, has_side_effects=True),
    )(source, near, basis, lifts, far_high, far_low)


def body(rhs, contrast, occupied, near, basis, transfer, coupling):
    shape = rhs.shape
    side, _, fields, parts, voxels = shape
    width = parts * voxels
    rank = basis.shape[1]
    levels = transfer.shape[0] + 1
    devices_x = lax.axis_size("gx")
    devices_y = lax.axis_size("gy")
    count = float(side * side * devices_x * devices_y * width)
    rhs = rhs.reshape(side, side, fields, width)
    weight = occupied.astype(jnp.float32)[:, :, None] * contrast
    weight = jnp.tile(weight, (1, 1, parts))[:, :, None, :]
    lifts = transfer.reshape(levels - 1, 4 * rank, rank)
    far_high, far_low = far_matrices(coupling)

    def operate(field):
        source = (weight * field).astype(jnp.bfloat16)
        source = jnp.pad(source, ((0, 0), (0, 0), (0, 8 - fields), (0, 0)))
        moved = apply(source, near, basis, lifts, far_high, far_low, devices_x, devices_y)
        return field + moved[:, :, :fields]

    def local_sum(one, other):
        return jnp.sum(one * other, axis=(0, 1, 3))

    def sums(*pairs):
        values = jnp.stack([local_sum(one, other) for one, other in pairs], axis=1)
        summed = sum_all(values, devices_x, devices_y)
        return [summed[:, i] for i in range(len(pairs))]

    def spread(values):
        return values[None, None, :, None]

    (square,) = sums((rhs, rhs))
    scale_start = jnp.sqrt(square / count + EPSILON)
    first = rhs / spread(scale_start)
    image = operate(first)
    total_proj, total_square = sums((first, image), (image, image))
    coef_first = total_proj / count
    norm_first = jnp.sqrt(total_square / count - coef_first * coef_first + EPSILON)
    second = (image - spread(coef_first) * first) / spread(norm_first)
    image = operate(second)
    total_cross, total_proj, total_square = sums((first, image), (second, image), (image, image))
    coef_cross = total_cross / count
    coef_second = total_proj / count
    rest = image - spread(coef_cross) * first - spread(coef_second) * second
    norm_second = jnp.sqrt(
        total_square / count - coef_cross * coef_cross - coef_second * coef_second + EPSILON
    )
    third = (rest / spread(norm_second)).reshape(shape)
    hess = jnp.stack(
        [scale_start, coef_first, norm_first, coef_cross, coef_second, norm_second], axis=1
    )
    return (third, hess)


def solution(mesh):
    placed = (
        P("gx", "gy", None, None, None),
        P("gx", "gy", None),
        P("gx", "gy"),
        P(),
        P(),
        P(),
        P(),
    )
    return jax.shard_map(
        body,
        mesh=mesh,
        in_specs=placed,
        out_specs=(P("gx", "gy", None, None, None), P()),
        check_vma=False,
    )
```

profile of v0, /device:TPU:0, one launch (start us, length us, event | category | flops | bytes accessed | tf_op | source)
XLA Modules:
  0.0 132.9 jit_solution(12650505330123484573)
XLA Ops:
  0.6 1.6 %multiply_reduce_fusion.5 = f32[6]{0:T(128)S(1)} fusion(f32[8,8,6,3,256]{4,1,3,2,0:T(8,128)} %param.7), kind=kLoop, calls=%fused_computation.12 | loop fusion | flops 589818 | bytes 1179672 | tf_op jit(solution)/shard_map/reduce_sum | solution.py:448
  2.2 0.1 copy.30
  2.3 0.6 pad.19.part
  2.9 11.8 %shard_map.86 = f32[8,128]{1,0:T(8,128)} custom-call(f32[8,128]{1,0:T(8,128)} %pad.19.part), custom_call_target="tpu_custom_call" | custom-call | tf_op jit(solution)/shard_map/pallas_call | solution.py:146
  14.8 0.8 add_sqrt_fusion.2
  15.6 0.7 convert_element_type.18
  16.3 0.9 broadcast_multiply_fusion
  17.2 0.0 copy-done.3
  17.2 0.8 copy.32.refs_2_
  18.0 0.5 multiply_convert_fusion.1
  18.5 1.0 pad.20.refs_0_
  19.5 8.7 %shard_map.87 = (bf16[5,2304,256]{2,1,0:T(8,128)(2,1)}, bf16[5,2304,256]{2,1,0:T(8,128)(2,1)}) custom-call(f32[5,20,64,64]{3,2,1,0:T(8,128)} %coupling.1), custom_call_target="tpu_custom_call" | custom-call | tf_op jit(solution)/shard_map/pallas_call | solution.py:72
  28.2 30.8 %shard_map.88 = f32[8,8,8,768]{3,2,1,0:T(8,128)} custom-call(bf16[8,8,8,768]{3,2,1,0:T(8,128)(2,1)} %pad.20.refs_0_, bf16[5,768,768]{2,1,0:T(8,128)(2,1)} %refs_1_.3, bf16[768,64]{1,0:T(8,128)(2,1)} %copy.32.refs_2_, f32[4,256,64]{2,1,0:T(8,128)} %bitcast.14, bf16[5,2304,256]{2,1,0:T(8,128)(2,1)} %get-tuple-element.4.refs_4_, ...), custom_call_target="tpu_custom_call" | custom-call | tf_op jit(solution)/shard_map/pallas_call | solution.py:416
  59.0 2.3 %multiply_reduce_fusion.4 = (f32[6]{0:T(128)S(1)}, f32[6]{0:T(128)S(1)}) fusion(f32[8,8,8,768]{3,2,1,0:T(8,128)} %shard_map.88, f32[6]{0:T(128)S(1)} %get-tuple-element.30, f32[8,8,6,768]{3,1,2,0:T(8,128)S(1)} %bitcast.10), kind=kLoop, calls=%fused_computation.9 | loop fusion | flops 1769460 | bytes 2359368 | tf_op jit(solution)/shard_map/reduce_sum | solution.py:448
  61.3 0.1 copy.33
  61.4 0.6 pad.21.part
  62.0 12.3 %shard_map.89 = f32[8,128]{1,0:T(8,128)} custom-call(f32[8,128]{1,0:T(8,128)} %pad.21.part), custom_call_target="tpu_custom_call" | custom-call | tf_op jit(solution)/shard_map/pallas_call | solution.py:146
  74.4 1.0 fusion.3
  75.4 1.9 %multiply_convert_fusion = (bf16[8,8,6,768]{3,2,1,0:T(8,128)(2,1)S(1)}, f32[8,8,6,768]{3,2,1,0:T(8,128)}) fusion(f32[8,8,768]{2,1,0:T(8,128)S(1)} %bitcast.17, f32[6]{0:T(128)S(1)} %add_sqrt_fusion.4, f32[6]{0:T(128)S(1)} %get-tuple-element.20, f32[8,8,8,768]{3,2,1,0:T(8,128)S(1)} %copy-done.2, f32[6]{0:T(128)S(1)} %get-tuple-element.30, ...), kind=kLoop, calls=%fused_computation.6 | loop fusion | flops 2064384 | bytes 4325448 | tf_op jit(solution)/shard_map/convert_element_type | solution.py:442
  77.3 1.0 pad.22.refs_0_
  78.3 29.6 %shard_map.90 = f32[8,8,8,768]{3,2,1,0:T(8,128)} custom-call(bf16[8,8,8,768]{3,2,1,0:T(8,128)(2,1)} %pad.22.refs_0_, bf16[5,768,768]{2,1,0:T(8,128)(2,1)} %refs_1_.3, bf16[768,64]{1,0:T(8,128)(2,1)} %copy.32.refs_2_, f32[4,256,64]{2,1,0:T(8,128)} %bitcast.15, bf16[5,2304,256]{2,1,0:T(8,128)(2,1)} %get-tuple-element.4.refs_4_, ...), custom_call_target="tpu_custom_call" | custom-call | tf_op jit(solution)/shard_map/pallas_call | solution.py:416
  107.8 2.8 %multiply_reduce_fusion.2 = (f32[6]{0:T(128)S(1)}, f32[6]{0:T(128)S(1)}, f32[6]{0:T(128)S(1)}) fusion(f32[8,8,6,768]{3,2,1,0:T(8,128)} %get-tuple-element.23, f32[8,8,8,768]{3,2,1,0:T(8,128)} %shard_map.90, f32[6]{0:T(128)S(1)} %get-tuple-element.30, f32[8,8,6,768]{3,1,2,0:T(8,128)S(1)} %bitcast.12), kind=kLoop, calls=%fused_computation.4 | loop fusion | flops 2359278 | bytes 3539040 | tf_op jit(solution)/shard_map/reduce_sum | solution.py:448
  110.7 0.1 copy.37
  110.8 0.1 copy.35
  110.8 0.1 copy.36
  110.9 0.7 select_maximum_fusion.part
  111.6 12.5 %shard_map.91 = f32[8,128]{1,0:T(8,128)} custom-call(f32[8,128]{1,0:T(8,128)} %select_maximum_fusion.part), custom_call_target="tpu_custom_call" | custom-call | tf_op jit(solution)/shard_map/pallas_call | solution.py:146
  124.2 1.0 fusion.4
  125.2 0.7 stack.41
  125.9 3.2 %subtract_divide_fusion = f32[8,8,6,768]{3,2,1,0:T(8,128)} fusion(f32[8,8,6,768]{3,2,1,0:T(8,128)} %get-tuple-element.23, f32[6]{0:T(128)S(1)} %add_sqrt_fusion.3, f32[6]{0:T(128)S(1)} %get-tuple-element.18, f32[6]{0:T(128)S(1)} %get-tuple-element.17, f32[8,8,8,768]{3,2,1,0:T(8,128)S(1)} %copy-done.1, f32[6]{0:T(128)S(1)} %get-tuple-element.30, ...), kind=kLoop, calls=%fused_computation.1 | loop fusion | flops 2064384 | bytes 4718688 | tf_op jit(solution)/shard_map/div | solution.py:474
  129.1 2.4 %reshape.89 = f32[8,8,6,3,256]{4,3,2,1,0:T(4,128)S(1)} reshape(f32[8,8,6,768]{3,2,1,0:T(8,128)} %subtract_divide_fusion) | data formatting | bytes 2359296 | tf_op jit(solution)/shard_map/reshape | solution.py:474
  131.5 1.4 %copy.39 = f32[8,8,6,3,256]{4,1,3,2,0:T(8,128)} copy(f32[8,8,6,3,256]{4,3,2,1,0:T(4,128)S(1)} %reshape.89) | data formatting | bytes 2359296
  (11 shorter events, 0.1 us)
Async XLA Ops:
  0.6 17.4 %copy-start = (f32[8,8,6,3,256]{4,1,3,2,0:T(8,128)S(1)}, f32[8,8,6,3,256]{4,1,3,2,0:T(8,128)}, u32[]{:S(2)}) copy-start(f32[8,8,6,3,256]{4,1,3,2,0:T(8,128)} %param.7) | copy-start | bytes 3538948
  0.6 16.5 %copy-start.3 = (bf16[768,64]{0,1:T(8,128)(2,1)S(1)}, bf16[768,64]{0,1:T(8,128)(2,1)}, u32[]{:S(2)}) copy-start(bf16[768,64]{0,1:T(8,128)(2,1)} %param.11) | copy-start | bytes 294916
  59.0 16.3 %copy-start.2 = (f32[8,8,8,768]{3,2,1,0:T(8,128)S(1)}, f32[8,8,8,768]{3,2,1,0:T(8,128)}, u32[]{:S(2)}) copy-start(f32[8,8,8,768]{3,2,1,0:T(8,128)} %shard_map.88) | copy-start | bytes 4718596
  107.8 18.0 %copy-start.1 = (f32[8,8,8,768]{3,2,1,0:T(8,128)S(1)}, f32[8,8,8,768]{3,2,1,0:T(8,128)}, u32[]{:S(2)}) copy-start(f32[8,8,8,768]{3,2,1,0:T(8,128)} %shard_map.90) | copy-start | bytes 4718596
where the time goes:
time: 133 us
  Pallas kernels  106 us (80%)
  other arithmetic  17.4 us (13%)
  local copies, waits for them, and re-layouts  9.02 us (7%)
    pallas_call x2, Pallas kernels, apply(): pl.pallas_call(functools.partial(operate_kernel, size_x, size_y, inner),...  60.3 us
    pallas_call x3, Pallas kernels, sum_all(): pl.pallas_call(functools.partial(sum_kernel, size_x, size_y), in_specs=[V...  36.7 us
    pallas_call x1, Pallas kernels, far_matrices(): pl.pallas_call(far_kernel, grid=(levels,), in_specs=[pl.BlockSpec((1, slo...  8.71 us
    reduce_sum x3, other arithmetic, local_sum(): return jnp.sum(one * other, axis=(0, 1, 3))  6.66 us
    div x1, other arithmetic, body(): third = (rest / spread(norm_second)).reshape(shape)  3.2 us

commit v1 on v0

v1 whole, which is shorter than its diff:
```python
import functools

import jax
import jax.numpy as jnp
from jax import lax
from jax.experimental import pallas as pl
from jax.experimental.pallas import tpu as pltpu
from jax.sharding import PartitionSpec as P

EPSILON = 1e-06
NEAR_BASE = ((0, 0), (1, -1), (1, 0), (1, 1), (0, 1))
AROUND = [(a, b) for a in (-1, 0, 1) for b in (-1, 0, 1)]
COMPASS = [d for d in AROUND if d != (0, 0)]
MESH = pl.DeviceIdType.MESH
VMEM = pl.BlockSpec(memory_space=pltpu.VMEM)


def near_lookup():
    table = {}
    for slot, (a, b) in enumerate(NEAR_BASE):
        table[(a, b)] = (slot, False)
        if (a, b) != (0, 0):
            table[(-a, -b)] = (slot, True)
    return table


def far_lookup():
    base = [
        (a, b)
        for a in range(-3, 4)
        for b in range(-3, 4)
        if max(abs(a), abs(b)) >= 2 and (a > 0 or (a == 0 and b > 0))
    ]
    table = {}
    for slot, (a, b) in enumerate(base):
        table[(a, b)] = (slot, False)
        table[(-a, -b)] = (slot, True)
    return table


def halves(values):
    high = values.astype(jnp.bfloat16)
    return high, (values - high.astype(jnp.float32)).astype(jnp.bfloat16)


def far_level(depth, coupling, high, low):
    table = far_lookup()
    rank = coupling.shape[2]
    children = [(c, e) for c in (0, 1) for e in (0, 1)]
    empty = jnp.zeros((rank, rank), jnp.float32)
    row = 0
    for px, py in AROUND:
        for c, e in children:
            line = []
            for tc, te in children:
                found = table.get((2 * px + c - tc, 2 * py + e - te))
                if found is None:
                    line.append(empty)
                else:
                    block = coupling[depth, found[0]]
                    line.append(block.T if found[1] else block)
            high[depth, row : row + rank, :], low[depth, row : row + rank, :] = halves(
                jnp.concatenate(line, axis=1)
            )
            row += rank


def place(index, size_y):
    return {"gx": index // size_y, "gy": index % size_y}


def greet_all(size_x, size_y):
    total = size_x * size_y
    me = lax.axis_index("gx") * size_y + lax.axis_index("gy")
    barrier = pltpu.get_barrier_semaphore()

    def greet(step, carry):
        other = (me + step) % total
        pl.semaphore_signal(
            barrier, inc=1, device_id=place(other, size_y), device_id_type=MESH
        )
        return carry

    lax.fori_loop(1, total, greet, 0)


def await_greetings(size_x, size_y):
    pl.semaphore_wait(pltpu.get_barrier_semaphore(), size_x * size_y - 1)


def gather_copy(source, target, send, receive, step, size_x, size_y):
    total = size_x * size_y
    me = lax.axis_index("gx") * size_y + lax.axis_index("gy")
    other = (me + step) % total
    return pltpu.make_async_remote_copy(
        src_ref=source,
        dst_ref=target.at[me],
        send_sem=send.at[step],
        recv_sem=receive.at[step],
        device_id=place(other, size_y),
        device_id_type=MESH,
    )


def strip(move, length):
    if move > 0:
        return pl.ds(length, 1), pl.ds(0, 1)
    if move < 0:
        return pl.ds(1, 1), pl.ds(length + 1, 1)
    return pl.ds(1, length), pl.ds(1, length)


def stacked(values):
    high = values.astype(jnp.bfloat16).astype(jnp.float32)
    return jnp.concatenate([high, values - high], axis=0).astype(jnp.bfloat16)


def product(left, right, across=1):
    return lax.dot_general(
        left, right, (((1,), (1 - across,)), ((), ())), preferred_element_type=jnp.float32
    )


def times(values, high, low, across=1):
    both = stacked(values)
    total = product(both, high, across) + product(both, low, across)
    rows = values.shape[0]
    return total[:rows] + total[rows:]


def group(boxes, size_x, size_y):
    rows = []
    for x in range(0, size_x, 2):
        for y in range(0, size_y, 2):
            four = [(x + c) * size_y + y + e for c in (0, 1) for e in (0, 1)]
            rows.append(jnp.concatenate([boxes[8 * i : 8 * i + 8] for i in four], axis=1))
    return rows


def ungroup(parents, size_x, size_y):
    rank = parents.shape[1] // 4
    rows = []
    for x in range(2 * size_x):
        for y in range(2 * size_y):
            i = (x // 2) * size_y + y // 2
            k = 2 * (x % 2) + y % 2
            rows.append(parents[8 * i : 8 * i + 8, k * rank : (k + 1) * rank])
    return jnp.concatenate(rows, axis=0)


def clear_rim(out):
    long_x, long_y = out.shape[0], out.shape[1]
    line_x = jnp.zeros((1,) + out.shape[1:], out.dtype)
    line_y = jnp.zeros((long_x, 1) + out.shape[2:], out.dtype)
    out[0:1] = line_x
    out[long_x - 1 : long_x] = line_x
    out[:, 0:1] = line_y
    out[:, long_y - 1 : long_y] = line_y


def krylov_kernel(size_x, size_y, inner, count, *refs):
    rhs, weight, near_far_away, basis, lifts, coupling, third, hess = refs[:8]
    near, far_high, far_low, first, second, source = refs[8:14]
    padded = refs[14]
    pyramid = refs[15 : 15 + inner]
    rest = refs[15 + inner :]
    coarse = coupling.shape[0] - inner
    tops = rest[:coarse]
    mine, gathered, shifted, total, parts, slots = rest[coarse : coarse + 6]
    send, receive, gather_send, gather_receive, sum_send, sum_receive, load = rest[coarse + 6 :]
    side = source.shape[0]
    width = source.shape[3]
    rank = basis.shape[1]
    devices = size_x * size_y
    me_x, me_y = lax.axis_index("gx"), lax.axis_index("gy")
    me = me_x * size_y + me_y
    ways = range(len(COMPASS))
    bands = (padded,) + tuple(pyramid)
    rows = side * side * 8
    lane = lax.broadcasted_iota(jnp.int32, (8, 128), 1)

    def tile_of(columns):
        tile = jnp.zeros((8, 128), jnp.float32)
        for i, column in enumerate(columns):
            tile = jnp.where(lane == i, column, tile)
        return tile

    def start_sums(number, sums):
        tile = tile_of([jnp.sum(value, axis=1, keepdims=True) for value in sums])
        parts[number] = tile
        slots[number, me] = tile

        def begin(step, carry):
            gather_copy(
                parts.at[number],
                slots.at[number],
                sum_send.at[number],
                sum_receive.at[number],
                step,
                size_x,
                size_y,
            ).start()
            return carry

        lax.fori_loop(1, devices, begin, 0)

    def finish_gather(piece, target, sent, received):
        def finish(step, carry):
            other = (me + devices - step) % devices
            pltpu.make_async_remote_copy(
                src_ref=piece,
                dst_ref=target.at[other],
                send_sem=sent.at[step],
                recv_sem=received.at[step],
                device_id=place((me + step) % devices, size_y),
                device_id_type=MESH,
            ).wait()
            return carry

        lax.fori_loop(1, devices, finish, 0)

    def finish_sums(number, amount):
        finish_gather(
            parts.at[number], slots.at[number], sum_send.at[number], sum_receive.at[number]
        )
        tile = jnp.sum(slots[number], axis=0) / count
        return [tile[:, i : i + 1] for i in range(amount)]

    def rows_sum(value):
        return jnp.sum(value, axis=0)

    def sweep(amount, work):
        def one(x, sums):
            return tuple(old + new for old, new in zip(sums, work(x)))

        return lax.fori_loop(0, side, one, (jnp.zeros((8, width), jnp.float32),) * amount)

    near_copy = pltpu.make_async_copy(near_far_away, near, load.at[0])
    near_copy.start()
    for band in bands + tuple(tops):
        clear_rim(band)
    greet_all(size_x, size_y)
    sums = sweep(1, lambda x: (rows_sum(rhs[x] * rhs[x]),))
    await_greetings(size_x, size_y)
    start_sums(0, sums)

    def build(depth, carry):
        far_level(depth, coupling, far_high, far_low)
        return carry

    lax.fori_loop(0, coupling.shape[0], build, 0)
    (square,) = finish_sums(0, 1)
    beta = jnp.sqrt(square + EPSILON)

    def copy_of(number, way):
        move_x, move_y = COMPASS[way]
        band = bands[number]
        from_x, to_x = strip(move_x, band.shape[0] - 2)
        from_y, to_y = strip(move_y, band.shape[1] - 2)
        return pltpu.make_async_remote_copy(
            src_ref=band.at[from_x, from_y],
            dst_ref=band.at[to_x, to_y],
            send_sem=send.at[number, way],
            recv_sem=receive.at[number, way],
            device_id={"gx": me_x + move_x, "gy": me_y + move_y},
            device_id_type=MESH,
        )

    def inside(place_x, place_y):
        return (place_x >= 0) & (place_x < size_x) & (place_y >= 0) & (place_y < size_y)

    def start_bands(numbers):
        for way in ways:
            move_x, move_y = COMPASS[way]

            @pl.when(inside(me_x + move_x, me_y + move_y))
            def _(way=way):
                for number in numbers:
                    copy_of(number, way).start()

    def finish_bands(numbers):
        for way in ways:
            move_x, move_y = COMPASS[way]

            @pl.when(inside(me_x + move_x, me_y + move_y))
            def _(way=way):
                for number in numbers:
                    copy_of(number, way).wait_send()

            @pl.when(inside(me_x - move_x, me_y - move_y))
            def _(way=way):
                for number in numbers:
                    copy_of(number, way).wait_recv()

    def operate():
        padded[1 : 1 + side, 1 : 1 + side] = source[...]
        start_bands((0,))

        flat = source[...].astype(jnp.float32).reshape(side * side * 8, width).astype(jnp.bfloat16)
        level = product(flat, basis[...])
        span = side
        for depth in range(inner):
            parents = group(level, span, span)
            span //= 2
            for i, parent in enumerate(parents):
                pyramid[depth][1 + i // span, 1 + i % span] = parent
            high, low = halves(lifts[depth])
            level = times(jnp.concatenate(parents, axis=0), high, low)
        mine[...] = level
        gathered[me] = level
        start_bands(range(1, inner + 1))

        def begin(step, carry):
            gather_copy(mine, gathered, gather_send, gather_receive, step, size_x, size_y).start()
            return carry

        lax.fori_loop(1, devices, begin, 0)

        finish_bands((0,))
        for b in range(3):
            shifted[b] = (
                padded[:, b : b + side]
                .astype(jnp.float32)
                .reshape((side + 2) * side * 8, width)
                .astype(jnp.bfloat16)
            )
        table = near_lookup()
        chunk = 256 if width % 256 == 0 else 128

        def near_columns(index, carry):
            columns = pl.ds(pl.multiple_of(index * chunk, chunk), chunk)
            value = jnp.zeros((rows, chunk), jnp.float32)
            for a, b in AROUND:
                slot, flipped = table[(a, b)]
                piece = shifted[1 + b, (1 + a) * side * 8 : (1 + a) * side * 8 + rows]
                if flipped:
                    value = value + product(piece, near[slot, columns, :], 0)
                else:
                    value = value + product(piece, near[slot, :, columns])
            total[:, columns] = value
            return carry

        lax.fori_loop(0, width // chunk, near_columns, 0)
        finish_bands(range(1, inner + 1))

        finish_gather(mine, gathered, gather_send, gather_receive)

        def couple(depth, window):
            value = None
            for k, (a, b) in enumerate(AROUND):
                span_rows = slice(4 * rank * k, 4 * rank * (k + 1))
                term = times(window(a, b), far_high[depth, span_rows], far_low[depth, span_rows])
                value = term if value is None else value + term
            return value

        across, along = size_x, size_y
        boxes = gathered[...].reshape(devices * 8, rank)
        for step in range(coarse):
            parents = group(boxes, across, along)
            across, along = across // 2, along // 2
            for i, parent in enumerate(parents):
                tops[step][1 + i // along, 1 + i % along] = parent
            if step < coarse - 1:
                high, low = halves(lifts[inner + step])
                boxes = times(jnp.concatenate(parents, axis=0), high, low)
        down = None
        for step in range(coarse - 1, -1, -1):
            near_x, near_y = me_x >> step + 1, me_y >> step + 1
            value = couple(
                inner + step, lambda a, b: tops[step][near_x + (1 + a), near_y + (1 + b)]
            )
            if down is not None:
                high, low = halves(lifts[inner + step])
                value = value + times(down, high, low, 0)
            child = 2 * (me_x >> step & 1) + (me_y >> step & 1)
            down = jnp.zeros((8, rank), jnp.float32)
            for i in range(4):
                down = jnp.where(child == i, value[:, i * rank : (i + 1) * rank], down)

        span = 1
        for depth in range(inner - 1, -1, -1):
            band = pyramid[depth]
            value = couple(
                depth,
                lambda a, b: band[1 + a : 1 + a + span, 1 + b : 1 + b + span].reshape(
                    span * span * 8, 4 * rank
                ),
            )
            high, low = halves(lifts[depth])
            value = value + times(down, high, low, 0)
            down = ungroup(value, span, span)
            span *= 2
        spread_down = product(stacked(down), basis[...], 0)
        total[...] = total[...] + spread_down[:rows] + spread_down[rows:]

    boxes_of = side * 8

    def image_of(x, field):
        return field[x] + total[pl.ds(pl.multiple_of(x * boxes_of, 8), boxes_of)].reshape(
            side, 8, width
        )

    def set_first(x, carry):
        value = rhs[x] * inverse
        first[x] = value
        source[x] = (weight[x] * value).astype(jnp.bfloat16)
        return carry

    inverse = 1.0 / beta
    lax.fori_loop(0, side, set_first, 0)
    near_copy.wait()
    operate()

    def first_sums(x):
        value, image = first[x], image_of(x, first)
        second[x] = image
        return rows_sum(value * image), rows_sum(image * image)

    start_sums(1, sweep(2, first_sums))
    h11, square = finish_sums(1, 2)
    h21 = jnp.sqrt(square - h11 * h11 + EPSILON)
    inverse_second = 1.0 / h21

    def set_second(x, carry):
        value = (second[x] - h11 * first[x]) * inverse_second
        second[x] = value
        source[x] = (weight[x] * value).astype(jnp.bfloat16)
        return carry

    lax.fori_loop(0, side, set_second, 0)
    operate()

    def second_sums(x):
        image = image_of(x, second)
        third[x] = image
        return rows_sum(first[x] * image), rows_sum(second[x] * image), rows_sum(image * image)

    start_sums(2, sweep(3, second_sums))
    h12, h22, square = finish_sums(2, 3)
    h32 = jnp.sqrt(square - h12 * h12 - h22 * h22 + EPSILON)
    inverse_third = 1.0 / h32

    def set_third(x, carry):
        third[x] = (third[x] - h12 * first[x] - h22 * second[x]) * inverse_third
        return carry

    lax.fori_loop(0, side, set_third, 0)
    hess[...] = tile_of([beta, h11, h21, h12, h22, h32])


def krylov(rhs, weight, near, basis, lifts, coupling, count, size_x, size_y):
    side, _, _, width = rhs.shape
    rank = basis.shape[1]
    inner = side.bit_length() - 1
    levels = coupling.shape[0]
    coarse = levels - inner
    devices = size_x * size_y
    halos = inner + 1
    scratch = [
        pltpu.VMEM(near.shape, near.dtype),
        pltpu.VMEM((levels, 36 * rank, 4 * rank), jnp.bfloat16),
        pltpu.VMEM((levels, 36 * rank, 4 * rank), jnp.bfloat16),
        pltpu.VMEM(rhs.shape, jnp.float32),
        pltpu.VMEM(rhs.shape, jnp.float32),
        pltpu.VMEM(rhs.shape, jnp.bfloat16),
        pltpu.VMEM((side + 2, side + 2, 8, width), jnp.bfloat16),
    ]
    for depth in range(inner):
        span = (side >> depth + 1) + 2
        scratch.append(pltpu.VMEM((span, span, 8, 4 * rank), jnp.float32))
    for step in range(coarse):
        grid = ((size_x >> step + 1) + 2, (size_y >> step + 1) + 2)
        scratch.append(pltpu.VMEM(grid + (8, 4 * rank), jnp.float32))
    scratch += [
        pltpu.VMEM((8, rank), jnp.float32),
        pltpu.VMEM((devices, 8, rank), jnp.float32),
        pltpu.VMEM((3, (side + 2) * side * 8, width), jnp.bfloat16),
        pltpu.VMEM((side * side * 8, width), jnp.float32),
        pltpu.VMEM((3, 8, 128), jnp.float32),
        pltpu.VMEM((3, devices, 8, 128), jnp.float32),
        pltpu.SemaphoreType.DMA((halos, len(COMPASS))),
        pltpu.SemaphoreType.DMA((halos, len(COMPASS))),
        pltpu.SemaphoreType.DMA((devices,)),
        pltpu.SemaphoreType.DMA((devices,)),
        pltpu.SemaphoreType.DMA((3, devices)),
        pltpu.SemaphoreType.DMA((3, devices)),
        pltpu.SemaphoreType.DMA((1,)),
    ]
    return pl.pallas_call(
        functools.partial(krylov_kernel, size_x, size_y, inner, count),
        in_specs=[VMEM, VMEM, pl.BlockSpec(memory_space=pl.ANY), VMEM, VMEM, VMEM],
        out_specs=[VMEM, VMEM],
        out_shape=[
            jax.ShapeDtypeStruct(rhs.shape, jnp.float32),
            jax.ShapeDtypeStruct((8, 128), jnp.float32),
        ],
        scratch_shapes=scratch,
        compiler_params=pltpu.CompilerParams(collective_id=0, has_side_effects=True),
    )(rhs, weight, near, basis, lifts, coupling)


def body(rhs, contrast, occupied, near, basis, transfer, coupling):
    shape = rhs.shape
    side, _, fields, parts, voxels = shape
    width = parts * voxels
    rank = basis.shape[1]
    devices_x = lax.axis_size("gx")
    devices_y = lax.axis_size("gy")
    count = float(side * side * devices_x * devices_y * width)
    flat = rhs.reshape(side, side, fields, width)
    flat = jnp.pad(flat, ((0, 0), (0, 0), (0, 8 - fields), (0, 0)))
    weight = occupied.astype(jnp.float32)[:, :, None] * contrast
    weight = jnp.tile(weight, (1, 1, parts))[:, :, None, :]
    lifts = transfer.reshape(transfer.shape[0], 4 * rank, rank)
    third, hess = krylov(
        flat, weight, near, basis, lifts, coupling, count, devices_x, devices_y
    )
    return (third[:, :, :fields].reshape(shape), hess[:fields, :6])


def solution(mesh):
    placed = (
        P("gx", "gy", None, None, None),
        P("gx", "gy", None),
        P("gx", "gy"),
        P(),
        P(),
        P(),
        P(),
    )
    return jax.shard_map(
        body,
        mesh=mesh,
        in_specs=placed,
        out_specs=(P("gx", "gy", None, None, None), P()),
        check_vma=False,
    )
```

time: 133 us -> 84.5 us (0.64)
  Pallas kernels: 106 us -> 73.1 us
  other arithmetic: 17.4 us -> 1.7 us
    pallas_call x6 -> x1, Pallas kernels: 106 us -> 73.1 us  [krylov(): pl.pallas_call(functools.partial(krylov_kernel, size_x, size_y, inner, co...]
    reduce_sum x3 -> x0, other arithmetic: 6.66 us -> none  [local_sum(): return jnp.sum(one * other, axis=(0, 1, 3))]
    div x3 -> x0, other arithmetic: 5.19 us -> none  [the longest x1 3.2 us: body(): third = (rest / spread(norm_second)).reshape(shape)]
    convert_element_type x2 -> x0, other arithmetic: 2.38 us -> none  [operate(): source = (weight * field).astype(jnp.bfloat16)]
    pad x4 -> x1, local copies, waits for them, and re-layouts: 3.25 us -> 1.32 us  [body(): flat = jnp.pad(flat, ((0, 0), (0, 0), (0, 8 - fields), (0, 0)))]
    unnamed x10 -> x7, local copies, waits for them, and re-layouts: 2.2 us -> 3.68 us
    reshape x1 -> x2, local copies, waits for them, and re-layouts: 2.41 us -> 2.8 us  [the longest x1 2.42 us: body(): return (third[:, :, :fields].reshape(shape), hess[:fields, :6])]
where the time goes in v1:
time: 84.5 us; the launch traced here: 84.3 us
  Pallas kernels  73.1 us (87%)
  local copies, waits for them, and re-layouts  8.79 us (10%)
  other arithmetic  1.7 us (2%)
    pallas_call x1, Pallas kernels, krylov(): pl.pallas_call(functools.partial(krylov_kernel, size_x, size_y, inner, co...  73.1 us
    unnamed x7, local copies, waits for them, and re-layouts  3.68 us
    reshape x1, local copies, waits for them, and re-layouts, body(): return (third[:, :, :fields].reshape(shape), hess[:fields, :6])  2.42 us

profile of v1, /device:TPU:0, one launch (start us, length us, event | category | flops | bytes accessed | tf_op | source)
XLA Modules:
  0.0 84.3 jit_solution(13602029314590319642)
XLA Ops:
  0.6 0.0 copy-start
  0.6 0.8 convert_element_type.5
  1.4 0.9 %broadcast_multiply_fusion = f32[8,8,256]{2,1,0:T(8,128)S(1)} fusion(f32[8,8,256]{2,1,0:T(8,128)} %param.8, f32[8,8]{1,0:T(8,128)S(1)} %convert_element_type.5), kind=kLoop, calls=%fused_computation | loop fusion | flops 16384 | bytes 131328 | tf_op jit(solution)/shard_map/mul | solution.py:512
  2.4 0.9 %tile.10.refs_1_ = f32[8,8,1,768]{3,2,1,0:T(1,128)} reshape(f32[8,8,3,256]{3,2,1,0:T(4,128)S(1)} %tile.8) | data formatting | bytes 393216 | tf_op jit(solution)/shard_map/tile | solution.py:513
  3.3 1.7 %copy.14.refs_3_ = bf16[768,64]{1,0:T(8,128)(2,1)} copy(bf16[768,64]{0,1:T(8,128)(2,1)} %param.11) | data formatting | bytes 196608 | tf_op args[4]
  5.1 0.0 copy-done
  5.1 0.4 copy.12
  5.4 1.3 %pad.4.refs_0_ = f32[8,8,8,768]{3,2,1,0:T(8,128)} pad(f32[8,8,6,768]{3,2,1,0:T(8,128)S(1)} %copy.12, f32[]{:T(128)} %constant.2.clone.1), padding=0_0x0_0x0_2x0_0 | pad | bytes 2752516 | tf_op jit(solution)/shard_map/jit(_pad)/pad | solution.py:511
  6.8 73.1 %shard_map.86 = (f32[8,8,8,768]{3,2,1,0:T(8,128)}, f32[8,128]{1,0:T(8,128)}) custom-call(f32[8,8,8,768]{3,2,1,0:T(8,128)} %pad.4.refs_0_, f32[8,8,1,768]{3,2,1,0:T(1,128)} %tile.10.refs_1_, bf16[5,768,768]{2,1,0:T(8,128)(2,1)} %refs_2_.1, bf16[768,64]{1,0:T(8,128)(2,1)} %copy.14.refs_3_, f32[4,256,64]{2,1,0:T(8,128)} %bitcast.6, f32[5,20,64,64]{3,2,1,0:T(8,128)} %refs_5_.1), custom_call_target="tpu_custom_call" | custom-call | tf_op jit(solution)/shard_map/pallas_call | solution.py:489
  79.9 2.4 %reshape.23 = f32[8,8,6,3,256]{4,3,2,1,0:T(4,128)S(1)} reshape(f32[8,8,6,768]{3,2,1,0:T(8,128)} %bitcast.4) | data formatting | bytes 2359296 | tf_op jit(solution)/shard_map/reshape | solution.py:518
  82.3 0.0 copy-start.1
  82.3 1.4 %copy.16 = f32[8,8,6,3,256]{4,1,3,2,0:T(8,128)} copy(f32[8,8,6,3,256]{4,3,2,1,0:T(4,128)S(1)} %reshape.23) | data formatting | bytes 2359296
  83.7 0.0 copy-done.1
  83.7 0.6 copy.20
  (1 shorter events, 0.0 us)
Async XLA Ops:
  0.6 4.4 %copy-start = (f32[8,8,6,3,256]{4,1,3,2,0:T(8,128)S(1)}, f32[8,8,6,3,256]{4,1,3,2,0:T(8,128)}, u32[]{:S(2)}) copy-start(f32[8,8,6,3,256]{4,1,3,2,0:T(8,128)} %param.7) | copy-start | bytes 3538948
  82.3 1.4 %copy-start.1 = (f32[8,128]{1,0:T(8,128)S(1)}, f32[8,128]{1,0:T(8,128)}, u32[]{:S(2)}) copy-start(f32[8,128]{1,0:T(8,128)} %get-tuple-element.5) | copy-start | bytes 12292

commit v2 on v1

--- a/solution.py
+++ b/solution.py
@@ -170,7 +170,7 @@
     send, receive, gather_send, gather_receive, sum_send, sum_receive, load = rest[coarse + 6 :]
     side = source.shape[0]
     width = source.shape[3]
-    rank = basis.shape[1]
+    rank = basis.shape[0]
     devices = size_x * size_y
     me_x, me_y = lax.axis_index("gx"), lax.axis_index("gy")
     me = me_x * size_y + me_y
@@ -297,7 +297,7 @@
         start_bands((0,))
 
         flat = source[...].astype(jnp.float32).reshape(side * side * 8, width).astype(jnp.bfloat16)
-        level = product(flat, basis[...])
+        level = product(flat, basis[...], 0)
         span = side
         for depth in range(inner):
             parents = group(level, span, span)
@@ -316,28 +316,51 @@
 
         lax.fori_loop(1, devices, begin, 0)
 
+        box_row = side * 8
+        shifted[1, box_row : box_row + rows] = flat
+        table = near_lookup()
+        chunk = 256 if width % 256 == 0 else 128
+
+        def near_term(a, b, columns, begin, end):
+            slot, flipped = table[(a, b)]
+            piece = shifted[1 + b, begin * box_row : end * box_row]
+            if flipped:
+                return product(piece, near[slot, columns, :], 0)
+            return product(piece, near[slot, :, columns])
+
+        def own_columns(index, carry):
+            columns = pl.ds(pl.multiple_of(index * chunk, chunk), chunk)
+            total[:, columns] = near_term(0, 0, columns, 1, side + 1)
+            total[: rows - box_row, columns] += near_term(1, 0, columns, 2, side + 1)
+            total[box_row:, columns] += near_term(-1, 0, columns, 1, side)
+            return carry
+
+        lax.fori_loop(0, width // chunk, own_columns, 0)
         finish_bands((0,))
-        for b in range(3):
+        for b in (0, 2):
             shifted[b] = (
                 padded[:, b : b + side]
                 .astype(jnp.float32)
                 .reshape((side + 2) * side * 8, width)
                 .astype(jnp.bfloat16)
             )
-        table = near_lookup()
-        chunk = 256 if width % 256 == 0 else 128
+        for x in (0, side + 1):
+            shifted[1, x * box_row : (x + 1) * box_row] = (
+                padded[x, 1 : 1 + side]
+                .astype(jnp.float32)
+                .reshape(box_row, width)
+                .astype(jnp.bfloat16)
+            )
 
         def near_columns(index, carry):
             columns = pl.ds(pl.multiple_of(index * chunk, chunk), chunk)
-            value = jnp.zeros((rows, chunk), jnp.float32)
-            for a, b in AROUND:
-                slot, flipped = table[(a, b)]
-                piece = shifted[1 + b, (1 + a) * side * 8 : (1 + a) * side * 8 + rows]
-                if flipped:
-                    value = value + product(piece, near[slot, columns, :], 0)
-                else:
-                    value = value + product(piece, near[slot, :, columns])
+            value = total[:, columns]
+            for a in (-1, 0, 1):
+                for b in (-1, 1):
+                    value = value + near_term(a, b, columns, 1 + a, 1 + a + side)
             total[:, columns] = value
+            total[rows - box_row :, columns] += near_term(1, 0, columns, side + 1, side + 2)
+            total[:box_row, columns] += near_term(-1, 0, columns, 0, 1)
             return carry
 
         lax.fori_loop(0, width // chunk, near_columns, 0)
@@ -390,7 +413,7 @@
             value = value + times(down, high, low, 0)
             down = ungroup(value, span, span)
             span *= 2
-        spread_down = product(stacked(down), basis[...], 0)
+        spread_down = product(stacked(down), basis[...])
         total[...] = total[...] + spread_down[:rows] + spread_down[rows:]
 
     boxes_of = side * 8
@@ -400,10 +423,13 @@
             side, 8, width
         )
 
+    def wide_weight(x):
+        return jnp.concatenate([weight[x]] * (width // weight.shape[3]), axis=-1)
+
     def set_first(x, carry):
         value = rhs[x] * inverse
         first[x] = value
-        source[x] = (weight[x] * value).astype(jnp.bfloat16)
+        source[x] = (wide_weight(x) * value).astype(jnp.bfloat16)
         return carry
 
     inverse = 1.0 / beta
@@ -424,7 +450,7 @@
     def set_second(x, carry):
         value = (second[x] - h11 * first[x]) * inverse_second
         second[x] = value
-        source[x] = (weight[x] * value).astype(jnp.bfloat16)
+        source[x] = (wide_weight(x) * value).astype(jnp.bfloat16)
         return carry
 
     lax.fori_loop(0, side, set_second, 0)
@@ -450,7 +476,7 @@
 
 def krylov(rhs, weight, near, basis, lifts, coupling, count, size_x, size_y):
     side, _, _, width = rhs.shape
-    rank = basis.shape[1]
+    rank = basis.shape[0]
     inner = side.bit_length() - 1
     levels = coupling.shape[0]
     coarse = levels - inner
@@ -510,10 +536,10 @@
     flat = rhs.reshape(side, side, fields, width)
     flat = jnp.pad(flat, ((0, 0), (0, 0), (0, 8 - fields), (0, 0)))
     weight = occupied.astype(jnp.float32)[:, :, None] * contrast
-    weight = jnp.tile(weight, (1, 1, parts))[:, :, None, :]
+    weight = weight[:, :, None, :]
     lifts = transfer.reshape(transfer.shape[0], 4 * rank, rank)
     third, hess = krylov(
-        flat, weight, near, basis, lifts, coupling, count, devices_x, devices_y
+        flat, weight, near, basis.T, lifts, coupling, count, devices_x, devices_y
     )
     return (third[:, :, :fields].reshape(shape), hess[:fields, :6])
 

time: 84.5 us -> 80.8 us (0.956)
  Pallas kernels: 73.1 us -> 70.1 us
    pallas_call x1, Pallas kernels: 73.1 us -> 70.1 us  [krylov(): pl.pallas_call(functools.partial(krylov_kernel, size_x, size_y, inner, co...]
    unnamed x7 -> x4, local copies, waits for them, and re-layouts: 3.68 us -> 1.97 us
    reshape x1, local copies, waits for them, and re-layouts: 0.38 us -> 1.65 us  [body(): flat = rhs.reshape(side, side, fields, width)]
    another operation x2 -> x0, local copies, waits for them, and re-layouts: 1 us -> none  [body(): weight = jnp.tile(weight, (1, 1, parts))[:, :, None, :]]
where the time goes in v2:
time: 80.8 us; the launch traced here: 80.4 us
  Pallas kernels  70.1 us (87%)
  local copies, waits for them, and re-layouts  8.02 us (10%)
  other arithmetic  1.6 us (2%)
    pallas_call x1, Pallas kernels, krylov(): pl.pallas_call(functools.partial(krylov_kernel, size_x, size_y, inner, co...  70.1 us
    reshape x1, local copies, waits for them, and re-layouts, body(): return (third[:, :, :fields].reshape(shape), hess[:fields, :6])  2.42 us
    unnamed x4, local copies, waits for them, and re-layouts  1.97 us
    reshape x1, local copies, waits for them, and re-layouts, body(): flat = rhs.reshape(side, side, fields, width)  1.65 us

profile of v2, /device:TPU:0, one launch (start us, length us, event | category | flops | bytes accessed | tf_op | source)
XLA Modules:
  0.0 80.4 jit_solution(8572414370324774448)
XLA Ops:
  0.6 0.7 convert_element_type.5
  1.3 0.9 %broadcast_multiply_fusion = f32[8,8,256]{2,1,0:T(8,128)S(1)} fusion(f32[8,8,256]{2,1,0:T(8,128)} %param.8, f32[8,8]{1,0:T(8,128)S(1)} %convert_element_type.5), kind=kLoop, calls=%fused_computation | loop fusion | flops 16384 | bytes 131328 | tf_op jit(solution)/shard_map/mul | solution.py:538
  2.2 0.7 broadcast_in_dim.4.refs_1_
  2.9 1.7 %copy.11 = f32[8,8,6,768]{3,2,1,0:T(8,128)S(1)} copy(f32[8,8,6,768]{3,1,2,0:T(8,128)} %bitcast.6) | data formatting | bytes 2359296 | tf_op jit(solution)/shard_map/reshape | solution.py:536
  4.6 1.3 %pad.4.refs_0_ = f32[8,8,8,768]{3,2,1,0:T(8,128)} pad(f32[8,8,6,768]{3,2,1,0:T(8,128)S(1)} %copy.11, f32[]{:T(128)} %constant.2.clone.1), padding=0_0x0_0x0_2x0_0 | pad | bytes 2752516 | tf_op jit(solution)/shard_map/jit(_pad)/pad | solution.py:537
  5.9 70.1 %shard_map.86 = (f32[8,8,8,768]{3,2,1,0:T(8,128)}, f32[8,128]{1,0:T(8,128)}) custom-call(f32[8,8,8,768]{3,2,1,0:T(8,128)} %pad.4.refs_0_, f32[8,8,1,256]{3,2,1,0:T(1,128)} %broadcast_in_dim.4.refs_1_, bf16[5,768,768]{2,1,0:T(8,128)(2,1)} %refs_2_.1, bf16[64,768]{1,0:T(8,128)(2,1)} %bitcast.8, f32[4,256,64]{2,1,0:T(8,128)} %bitcast.7, f32[5,20,64,64]{3,2,1,0:T(8,128)} %refs_5_.1), custom_call_target="tpu_custom_call" | custom-call | tf_op jit(solution)/shard_map/pallas_call | solution.py:515
  76.0 2.4 %reshape.17 = f32[8,8,6,3,256]{4,3,2,1,0:T(4,128)S(1)} reshape(f32[8,8,6,768]{3,2,1,0:T(8,128)} %bitcast.5) | data formatting | bytes 2359296 | tf_op jit(solution)/shard_map/reshape | solution.py:544
  78.4 0.0 copy-start
  78.5 1.4 %copy.13 = f32[8,8,6,3,256]{4,1,3,2,0:T(8,128)} copy(f32[8,8,6,3,256]{4,3,2,1,0:T(4,128)S(1)} %reshape.17) | data formatting | bytes 2359296
  79.8 0.0 copy-done
  79.8 0.6 copy.17
Async XLA Ops:
  78.4 1.4 %copy-start = (f32[8,128]{1,0:T(8,128)S(1)}, f32[8,128]{1,0:T(8,128)}, u32[]{:S(2)}) copy-start(f32[8,128]{1,0:T(8,128)} %get-tuple-element.5) | copy-start | bytes 12292

commit v3 on v2

--- a/solution.py
+++ b/solution.py
@@ -240,7 +240,16 @@
     for band in bands + tuple(tops):
         clear_rim(band)
     greet_all(size_x, size_y)
-    sums = sweep(1, lambda x: (rows_sum(rhs[x] * rhs[x]),))
+
+    def rhs_sums(x):
+        pieces = [jnp.swapaxes(rhs[x, :, part], 0, 1) for part in range(rhs.shape[2])]
+        value = jnp.concatenate(pieces, axis=-1)
+        blank = jnp.zeros((side, 8 - rhs.shape[1], width), jnp.float32)
+        value = jnp.concatenate([value, blank], axis=1)
+        first[x] = value
+        return (rows_sum(value * value),)
+
+    sums = sweep(1, rhs_sums)
     await_greetings(size_x, size_y)
     start_sums(0, sums)
 
@@ -427,7 +436,7 @@
         return jnp.concatenate([weight[x]] * (width // weight.shape[3]), axis=-1)
 
     def set_first(x, carry):
-        value = rhs[x] * inverse
+        value = first[x] * inverse
         first[x] = value
         source[x] = (wide_weight(x) * value).astype(jnp.bfloat16)
         return carry
@@ -475,8 +484,9 @@
 
 
 def krylov(rhs, weight, near, basis, lifts, coupling, count, size_x, size_y):
-    side, _, _, width = rhs.shape
-    rank = basis.shape[0]
+    side = rhs.shape[0]
+    rank, width = basis.shape
+    boxes = (side, side, 8, width)
     inner = side.bit_length() - 1
     levels = coupling.shape[0]
     coarse = levels - inner
@@ -486,9 +496,9 @@
         pltpu.VMEM(near.shape, near.dtype),
         pltpu.VMEM((levels, 36 * rank, 4 * rank), jnp.bfloat16),
         pltpu.VMEM((levels, 36 * rank, 4 * rank), jnp.bfloat16),
-        pltpu.VMEM(rhs.shape, jnp.float32),
-        pltpu.VMEM(rhs.shape, jnp.float32),
-        pltpu.VMEM(rhs.shape, jnp.bfloat16),
+        pltpu.VMEM(boxes, jnp.float32),
+        pltpu.VMEM(boxes, jnp.float32),
+        pltpu.VMEM(boxes, jnp.bfloat16),
         pltpu.VMEM((side + 2, side + 2, 8, width), jnp.bfloat16),
     ]
     for depth in range(inner):
@@ -517,7 +527,7 @@
         in_specs=[VMEM, VMEM, pl.BlockSpec(memory_space=pl.ANY), VMEM, VMEM, VMEM],
         out_specs=[VMEM, VMEM],
         out_shape=[
-            jax.ShapeDtypeStruct(rhs.shape, jnp.float32),
+            jax.ShapeDtypeStruct(boxes, jnp.float32),
             jax.ShapeDtypeStruct((8, 128), jnp.float32),
         ],
         scratch_shapes=scratch,
@@ -533,8 +543,7 @@
     devices_x = lax.axis_size("gx")
     devices_y = lax.axis_size("gy")
     count = float(side * side * devices_x * devices_y * width)
-    flat = rhs.reshape(side, side, fields, width)
-    flat = jnp.pad(flat, ((0, 0), (0, 0), (0, 8 - fields), (0, 0)))
+    flat = rhs.transpose(0, 2, 3, 1, 4)
     weight = occupied.astype(jnp.float32)[:, :, None] * contrast
     weight = weight[:, :, None, :]
     lifts = transfer.reshape(transfer.shape[0], 4 * rank, rank)

time: 80.8 us -> 77.7 us (0.962)
  local copies, waits for them, and re-layouts: 8.02 us -> 5.06 us
    reshape x1 -> x0, local copies, waits for them, and re-layouts: 1.65 us -> none  [body(): flat = rhs.reshape(side, side, fields, width)]
    pad x1 -> x0, local copies, waits for them, and re-layouts: 1.3 us -> none  [body(): flat = jnp.pad(flat, ((0, 0), (0, 0), (0, 8 - fields), (0, 0)))]
where the time goes in v3:
time: 77.7 us; the launch traced here: 77.4 us
  Pallas kernels  70.1 us (90%)
  local copies, waits for them, and re-layouts  5.06 us (7%)
  other arithmetic  1.6 us (2%)
    pallas_call x1, Pallas kernels, krylov(): pl.pallas_call(functools.partial(krylov_kernel, size_x, size_y, inner, co...  70.1 us
    reshape x1, local copies, waits for them, and re-layouts, body(): return (third[:, :, :fields].reshape(shape), hess[:fields, :6])  2.42 us
    unnamed x4, local copies, waits for them, and re-layouts  1.97 us

profile of v3, /device:TPU:0, one launch (start us, length us, event | category | flops | bytes accessed | tf_op | source)
XLA Modules:
  0.0 77.4 jit_solution(1479013570174681702)
XLA Ops:
  0.6 0.7 convert_element_type.3
  1.3 0.9 %broadcast_multiply_fusion = f32[8,8,256]{2,1,0:T(8,128)S(1)} fusion(f32[8,8,256]{2,1,0:T(8,128)} %param.8, f32[8,8]{1,0:T(8,128)S(1)} %convert_element_type.3), kind=kLoop, calls=%fused_computation | loop fusion | flops 16384 | bytes 131328 | tf_op jit(solution)/shard_map/mul | solution.py:547
  2.2 0.7 broadcast_in_dim.4.refs_1_
  2.9 70.1 %shard_map.86 = (f32[8,8,8,768]{3,2,1,0:T(8,128)}, f32[8,128]{1,0:T(8,128)}) custom-call(f32[8,6,3,8,256]{4,3,2,1,0:T(8,128)} %bitcast.6, f32[8,8,1,256]{3,2,1,0:T(1,128)} %broadcast_in_dim.4.refs_1_, bf16[5,768,768]{2,1,0:T(8,128)(2,1)} %refs_2_.1, bf16[64,768]{1,0:T(8,128)(2,1)} %bitcast.8, f32[4,256,64]{2,1,0:T(8,128)} %bitcast.7, f32[5,20,64,64]{3,2,1,0:T(8,128)} %refs_5_.1), custom_call_target="tpu_custom_call" | custom-call | tf_op jit(solution)/shard_map/pallas_call | solution.py:525
  73.0 2.4 %reshape.13 = f32[8,8,6,3,256]{4,3,2,1,0:T(4,128)S(1)} reshape(f32[8,8,6,768]{3,2,1,0:T(8,128)} %bitcast.5) | data formatting | bytes 2359296 | tf_op jit(solution)/shard_map/reshape | solution.py:553
  75.4 0.0 copy-start
  75.4 1.4 %copy.11 = f32[8,8,6,3,256]{4,1,3,2,0:T(8,128)} copy(f32[8,8,6,3,256]{4,3,2,1,0:T(4,128)S(1)} %reshape.13) | data formatting | bytes 2359296
  76.8 0.0 copy-done
  76.8 0.6 copy.15
Async XLA Ops:
  75.4 1.4 %copy-start = (f32[8,128]{1,0:T(8,128)S(1)}, f32[8,128]{1,0:T(8,128)}, u32[]{:S(2)}) copy-start(f32[8,128]{1,0:T(8,128)} %get-tuple-element.5) | copy-start | bytes 12292
